TPU v7x, 256 devices: a whole 4x4x8 slice. The times are simulated.
256 devices in a mesh: dp: 4 (over y), tensor: 16 (over x, z_hi, core), section: 4 (over z_lo).
Axes of the slice: x: 4, y: 4, z: 8 (z_hi: 2, z_lo: 4; z = z_hi * 4 + z_lo), core: 2. Of those that a mesh axis runs over, the one named last changes fastest.
Arguments:
- sent_grads: bfloat16 [4, 4, 2, 384, 8192], P('section', 'dp', None, 'tensor'), may hold values from -0.15917969 to 0.15917969
- attn_out: bfloat16 [4, 4, 2, 384, 8192], P('section', 'dp', None, None, 'tensor'), may hold values from -6 to 6
- b_order: int32 [4, 2], replicated, may hold values from 0 to 1, each once within a row
Outputs:
- grad_wo: bfloat16 [4, 8192, 8192], P('section', 'dp', 'tensor')
Inputs may be any that keep to these rules, and one draw needn't show every extreme that they name: Each row of b_order is a permutation of the 2 micro-batches.
All inputs are finite; a program needn't handle non-finite values.
Results may differ from a plain program's by a relative error of at most 0.013.
Values may be sent and summed in bfloat16 or wider, within the bound.
A program may use at most 128 MiB of HBM per device.

v0:
```python
import jax
import jax.numpy as jnp
from jax import lax
from jax.sharding import PartitionSpec as P


def from_behind(block, axis, distance):
    devices = range(lax.axis_size(axis))
    route = [((i - distance) % len(devices), i) for i in devices]
    return lax.ppermute(block, axis, route)


def contract(left_side, right_side):
    return lax.dot_general(
        left_side, right_side, (((0, 1), (0, 1)), ((), ())), preferred_element_type=jnp.float32
    )


def on_device(sent_grads, attn_out, b_order):
    sections = lax.axis_size("section")
    upper_index = (lax.axis_index("section") + 1) % sections
    order_row = lax.dynamic_index_in_dim(b_order, upper_index, 0, keepdims=False)
    received = from_behind(sent_grads[0, 0], "section", -1)
    micro_ids = jnp.arange(received.shape[0], dtype=jnp.int32)
    matches = order_row[None, :] == micro_ids[:, None]
    zero_value = jnp.zeros((), received.dtype)
    out_grads = jnp.sum(jnp.where(matches[:, :, None, None], received[None], zero_value), axis=1)
    whole_grads = lax.all_gather(out_grads, "tensor", axis=1, tiled=True)
    heads_local = attn_out[0, 0]
    out_sum = lax.psum_scatter(
        contract(whole_grads, heads_local).astype(jnp.bfloat16),
        "dp",
        scatter_dimension=0,
        tiled=True,
    )
    return out_sum[None]


def solution(mesh):
    placed = (
        P("section", "dp", None, "tensor", None),
        P("section", "dp", None, None, "tensor"),
        P(),
    )
    return jax.shard_map(
        on_device,
        mesh=mesh,
        in_specs=placed,
        out_specs=P("section", "dp", "tensor"),
        check_vma=False,
    )
```

profile of v0, /device:TPU:1, one launch (start us, length us, event | category | flops | bytes accessed | tf_op | source)
XLA Modules:
  0.0 271.2 jit_solution(11676067018698046515)
XLA Ops:
  6.5 0.0 copy-start
  6.5 0.0 all-gather.2.cloned.1.call-start
  6.5 5.2 %collective-permute-start = (bf16[2,24,8192]{2,1,0:T(8,128)(2,1)}, bf16[2,24,8192]{2,1,0:T(8,128)(2,1)S(1)}, u32[]{:S(2)}, u32[]{:S(2)}) collective-permute-start(bf16[2,24,8192]{2,1,0:T(8,128)(2,1)} %bitcast.8), channel_id=1, source_target_pairs={{1,0},{2,1},{3,2},{0,3},{5,4},{6,5},{7,6},{4,7},{9,8},{10,9},{11,1... | collective-permute-start | bytes 2359304 | tf_op jit(solution)/shard_map/ppermute | solution.py:10
  11.7 0.9 dynamic-slice_reduce_fusion
  12.6 15.7 %collective-permute-done = bf16[2,24,8192]{2,1,0:T(8,128)(2,1)S(1)} collective-permute-done((bf16[2,24,8192]{2,1,0:T(8,128)(2,1)}, bf16[2,24,8192]{2,1,0:T(8,128)(2,1)S(1)}, u32[]{:S(2)}, u32[]{:S(2)}) %collective-permute-start) | collective-permute-done | bytes 786464 | tf_op jit(solution)/shard_map/ppermute | solution.py:10
  28.2 1.3 select_reduce_fusion
  29.6 0.0 all-gather.2.cloned.1.call-update
  29.6 0.0 reduce-scatter.2.cloned.1.call-start
  29.6 143.6 %all-gather.2.cloned.1.call-done = bf16[2,384,8192]{2,1,0:T(8,128)(2,1)} async-done(((bf16[2,24,8192]{2,1,0:T(8,128)(2,1)}), bf16[2,384,8192]{2,1,0:T(8,128)(2,1)}) %all-gather.2.cloned.1.call-update) | async-done | bytes 12582928 | tf_op jit(solution)/shard_map/all_gather | solution.py:28
  173.2 0.0 copy-done
  173.2 13.7 %bitcast_convert_fusion = bf16[8192,512]{1,0:T(8,128)(2,1)} fusion(bf16[2,384,8192]{2,1,0:T(8,128)(2,1)} %all-gather.2.cloned.1.call-done, bf16[1,1,2,384,512]{4,3,2,1,0:T(8,128)(2,1)S(1)} %copy-done), kind=kOutput, calls=%fused_computation | convolution fusion | flops 6446645248 | bytes 21757952 | tf_op jit(solution)/shard_map/dot_general | solution.py:14
  186.9 0.0 reduce-scatter.2.cloned.1.call-update
  186.9 77.4 %reduce-scatter.2.cloned.1.call-done = bf16[2048,512]{1,0:T(8,128)(2,1)} async-done(((bf16[8192,512]{1,0:T(8,128)(2,1)}), bf16[2048,512]{1,0:T(8,128)(2,1)}) %reduce-scatter.2.cloned.1.call-update) | async-done | bytes 2097168 | tf_op jit(solution)/shard_map/reduce_scatter | solution.py:30
  (1 shorter events, 0.0 us)
Async XLA Ops:
  6.5 166.7 %copy-start = (bf16[1,1,2,384,512]{4,3,2,1,0:T(8,128)(2,1)S(1)}, bf16[1,1,2,384,512]{4,3,2,1,0:T(8,128)(2,1)}, u32[]{:S(2)}) copy-start(bf16[1,1,2,384,512]{4,3,2,1,0:T(8,128)(2,1)} %param.4) | copy-start | bytes 2359300
  6.5 166.7 %all-gather.2.cloned.1.call-start = ((), (), s32[]{:S(2)}) async-start(), calls=%async_computation.1 | async-start | bytes 13369344 | tf_op jit(solution)/shard_map/all_gather | solution.py:28
  6.5 21.7 %collective-permute-start = (bf16[2,24,8192]{2,1,0:T(8,128)(2,1)}, bf16[2,24,8192]{2,1,0:T(8,128)(2,1)S(1)}, u32[]{:S(2)}, u32[]{:S(2)}) collective-permute-start(bf16[2,24,8192]{2,1,0:T(8,128)(2,1)} %bitcast.8), channel_id=1, source_target_pairs={{1,0},{2,1},{3,2},{0,3},{5,4},{6,5},{7,6},{4,7},{9,8},{10,9},{11,1... | collective-permute-start | bytes 2359304 | tf_op jit(solution)/shard_map/ppermute | solution.py:10
  29.6 234.8 %reduce-scatter.2.cloned.1.call-start = ((), (), s32[]{:S(2)}) async-start(), calls=%async_computation.2 | async-start | bytes 10485760 | tf_op jit(solution)/shard_map/reduce_scatter | solution.py:30
Sparse Core Ops, SparseCore 0:
  29.7 143.4 all-gather.1
  187.0 77.2 reduce-scatter.1
where the time goes:
time: 271 us
  waiting for transfers between devices  237 us (87%)
  matrix products  13.7 us (5%)
  between operations  13.4 us (5%)
  starting transfers between devices  5.22 us (2%)
    all_gather x1, waiting for transfers between devices, on_device(): whole_grads = lax.all_gather(out_grads, 'tensor', axis=1, tiled=True)  144 us
    reduce_scatter x1, waiting for transfers between devices, on_device(): lax.psum_scatter(contract(whole_grads, heads_local).astype(jnp.bfloat16),...  77.4 us
    ppermute x1, waiting for transfers between devices, from_behind(): return lax.ppermute(block, axis, route)  15.7 us
    dot_general x1, matrix products, contract(): lax.dot_general(left_side, right_side, (((0, 1), (0, 1)), ((), ())), pref...  13.7 us
  transfers between devices with their start and end apart: 3, of which 3 were waited for; matrix products, arithmetic and copies ran while one was open for 0% of the time, Pallas kernels for 0%

commit v1 on v0

v1 whole, which is shorter than its diff:
```python
import jax
import jax.numpy as jnp
from jax import lax
from jax.experimental import pallas as pl
from jax.experimental.pallas import tpu as pltpu
from jax.sharding import PartitionSpec as P

MESH = pl.DeviceIdType.MESH
N_DP, N_TENSOR, N_SECTION = 4, 16, 4
PIECE = 48
ROWS = N_TENSOR * PIECE
COLS = 2048
HALF = COLS // 2
WIDTH = 512
TILE = 256


def wrap(value, size):
    return lax.rem(value + size, size)


def kernel(
    grads, heads, out, a_all, b_all, acc,
    own_b, s1s, s1r, x1s, x1r, x2s, x2r, dds, ddr, b1s, b1r, b2s, b2r,
):
    y = lax.axis_index("dp")
    t = lax.axis_index("tensor")
    s = lax.axis_index("section")
    x = lax.div(t, 4)
    h = lax.rem(lax.div(t, 2), 2)
    c = lax.rem(t, 2)
    down, up = wrap(s - 1, 4), wrap(s + 1, 4)
    to_h = [wrap(h + lax.div(3 - s, 3) + n, 2) for n in (0, 1)]
    from_h = [wrap(h + lax.div(s, 3) + n, 2) for n in (0, 1)]

    def tensor_of(xx, hh, cc):
        return xx * 4 + hh * 2 + cc

    def rows_of(replica, source):
        return pl.ds(pl.multiple_of((replica * N_TENSOR + source) * PIECE, 16), PIECE)

    x_right, x_left, x_far = wrap(x + 1, 4), wrap(x - 1, 4), wrap(x + 2, 4)
    right, left = tensor_of(x_right, h, c), tensor_of(x_left, h, c)
    sibling = tensor_of(x, h, 1 - c)
    y_up, y_down, y_far = wrap(y + 1, 4), wrap(y - 1, 4), wrap(y + 2, 4)

    barrier = pltpu.get_barrier_semaphore()

    def greet(device):
        pl.semaphore_signal(barrier, inc=1, device_id=device, device_id_type=MESH)

    for j in range(4):
        for n in (0, 1):
            greet({"dp": wrap(y - j, 4), "tensor": tensor_of(x, from_h[n], c), "section": up})
    for device in (right, left, sibling):
        greet({"tensor": device})
    for device in (y_up, y_down):
        greet({"dp": device})
    pl.semaphore_wait(barrier, 13)

    def remote(src, dst, send, recv, device):
        return pltpu.make_async_remote_copy(
            src_ref=src, dst_ref=dst, send_sem=send, recv_sem=recv,
            device_id=device, device_id_type=MESH,
        )

    sends = []

    def go(copy):
        copy.start()
        sends.append(copy)

    def stage1(p):
        j, n = p // 2, p % 2
        target = wrap(y + j, 4)
        return remote(
            grads.at[:, pl.ds(pl.multiple_of(target * COLS, COLS), COLS)],
            a_all.at[rows_of(y, t), :],
            s1s.at[p], s1r.at[p],
            {"dp": target, "tensor": tensor_of(x, to_h[n], c), "section": down},
        )

    def stored(p, xx, cc, half=None):
        j, n = p // 2, p % 2
        rows = rows_of(wrap(y - j, 4), tensor_of(xx, from_h[n], cc))
        return a_all.at[rows, :] if half is None else a_all.at[rows, pl.ds(half * HALF, HALF)]

    def hop1(p, way, xx):
        block = stored(p, xx, c)
        return remote(block, block, x1s.at[p, way], x1r.at[p, way], {"tensor": (right, left)[way]})

    def hop2(p, way, xx):
        block = stored(p, xx, c, way)
        return remote(block, block, x2s.at[p, way], x2r.at[p, way], {"tensor": (right, left)[way]})

    def across(p, kind, cc):
        xx = (x, x_left, x_right, x_far)[kind]
        block = stored(p, xx, cc)
        return remote(block, block, dds.at[p, kind], ddr.at[p, kind], {"tensor": sibling})

    def b_rows(replica, half=None):
        if half is None:
            return b_all.at[pl.ds(pl.multiple_of(replica * ROWS, ROWS), ROWS), :]
        return b_all.at[pl.ds(pl.multiple_of(replica * ROWS + half * (ROWS // 2), 128), ROWS // 2), :]

    def b_hop1(way, src, replica):
        return remote(src, b_rows(replica), b1s.at[way], b1r.at[way], {"dp": (y_up, y_down)[way]})

    def b_hop2(way, replica):
        block = b_rows(replica, way)
        return remote(block, block, b2s.at[way], b2r.at[way], {"dp": (y_up, y_down)[way]})

    def compute(j):
        replica = wrap(y - j, 4)
        rows = pl.ds(pl.multiple_of(replica * ROWS, ROWS), ROWS)

        def tile(m, carry):
            columns = pl.ds(pl.multiple_of(m * TILE, TILE), TILE)
            part = lax.dot_general(
                a_all[rows, columns], b_all[rows, :], (((0,), (0,)), ((), ())),
                preferred_element_type=jnp.float32,
            )
            if j == 0:
                acc[columns, :] = part
            elif j < 3:
                acc[columns, :] += part
            else:
                out[columns, :] = (acc[columns, :] + part).astype(out.dtype)
            return carry

        lax.fori_loop(0, COLS // TILE, tile, 0)

    for p in range(8):
        go(stage1(p))
    own = pltpu.make_async_copy(heads, b_rows(y), own_b)
    own.start()
    for way in (0, 1):
        go(b_hop1(way, heads, y))

    def first(p):
        stage1(p).wait_recv()
        go(hop1(p, 0, x))
        go(hop1(p, 1, x))
        go(across(p, 0, c))

    def second(p):
        hop1(p, 0, x_left).wait_recv()
        go(hop2(p, 0, x_left))
        go(across(p, 1, c))
        hop1(p, 1, x_right).wait_recv()
        go(hop2(p, 1, x_right))
        go(across(p, 2, c))

    def third(p):
        hop2(p, 0, x_far).wait_recv()
        hop2(p, 1, x_far).wait_recv()
        go(across(p, 3, c))

    def finish(j):
        for p in (2 * j, 2 * j + 1):
            for kind in range(4):
                across(p, kind, 1 - c).wait_recv()
        if j == 2:
            for way in (0, 1):
                b_hop2(way, y_far).wait_recv()
        compute(j)

    for step in range(11):
        if step < 8:
            first(step)
        if 1 <= step < 9:
            second(step - 1)
        if 2 <= step < 10:
            third(step - 2)
        if step == 3:
            own.wait()
            b_hop1(0, heads, y_down).wait_recv()
            go(b_hop2(0, y_down))
            b_hop1(1, heads, y_up).wait_recv()
            go(b_hop2(1, y_up))
        if step >= 4 and step % 2 == 0:
            finish((step - 4) // 2)
    for copy in sends:
        copy.wait_send()


def on_device(sent_grads, attn_out, b_order):
    s = lax.axis_index("section")
    order = lax.dynamic_index_in_dim(b_order, lax.rem(s + 1, N_SECTION), 0, keepdims=False)
    grads = sent_grads[0, 0].reshape(PIECE, N_DP * COLS)
    heads = attn_out[0, 0]
    in_slots = jnp.stack([jnp.where(order[k] == 0, heads[0], heads[1]) for k in range(2)])
    in_slots = in_slots.reshape(2, N_TENSOR, PIECE // 2, WIDTH).transpose(1, 0, 2, 3).reshape(ROWS, WIDTH)
    dma = pltpu.SemaphoreType.DMA
    result = pl.pallas_call(
        kernel,
        out_shape=jax.ShapeDtypeStruct((COLS, WIDTH), jnp.bfloat16),
        in_specs=[pl.BlockSpec(memory_space=pl.ANY)] * 2,
        out_specs=pl.BlockSpec(memory_space=pltpu.VMEM),
        scratch_shapes=[
            pltpu.VMEM((N_DP * ROWS, COLS), jnp.bfloat16),
            pltpu.VMEM((N_DP * ROWS, WIDTH), jnp.bfloat16),
            pltpu.VMEM((COLS, WIDTH), jnp.float32),
            dma, dma((8,)), dma((8,)), dma((8, 2)), dma((8, 2)), dma((8, 2)), dma((8, 2)),
            dma((8, 4)), dma((8, 4)), dma((2,)), dma((2,)), dma((2,)), dma((2,)),
        ],
        compiler_params=pltpu.CompilerParams(
            collective_id=0, has_side_effects=True, vmem_limit_bytes=48 * 2**20
        ),
    )(grads, in_slots)
    return result[None]


def solution(mesh):
    placed = (
        P("section", "dp", None, "tensor", None),
        P("section", "dp", None, None, "tensor"),
        P(),
    )
    return jax.shard_map(
        on_device,
        mesh=mesh,
        in_specs=placed,
        out_specs=P("section", "dp", "tensor"),
        check_vma=False,
    )
```

time: 271 us -> 88.4 us (0.33)
  waiting for transfers between devices: 237 us -> 0 us
  Pallas kernels: 0 us -> 83.1 us
  matrix products: 13.7 us -> 0 us
  between operations: 13.4 us -> 1.3 us
  starting transfers between devices: 5.22 us -> 0 us
    all_gather x1 -> x0, waiting for transfers between devices: 144 us -> none  [on_device(): whole_grads = lax.all_gather(out_grads, 'tensor', axis=1, tiled=True)]
    pallas_call x0 -> x1, Pallas kernels: none -> 83.1 us  [on_device(): pl.pallas_call(kernel, out_shape=jax.ShapeDtypeStruct((COLS, WIDTH), jnp....]
    reduce_scatter x1 -> x0, waiting for transfers between devices: 77.4 us -> none  [on_device(): lax.psum_scatter(contract(whole_grads, heads_local).astype(jnp.bfloat16),...]
    ppermute x1 -> x0, waiting for transfers between devices: 15.7 us -> none  [from_behind(): return lax.ppermute(block, axis, route)]
    dot_general x1 -> x0, matrix products: 13.7 us -> none  [contract(): lax.dot_general(left_side, right_side, (((0, 1), (0, 1)), ((), ())), pref...]
    ppermute x1 -> x0, starting transfers between devices: 5.17 us -> none  [from_behind(): return lax.ppermute(block, axis, route)]
  transfers between devices with their start and end apart: 3 -> 0, of which waited for: 3 -> 0; matrix products, arithmetic and copies ran while one was open for 0% -> 0% of each run, Pallas kernels for 0% -> 0%
where the time goes in v1:
time: 88.4 us; the launch traced here: 88.2 us
  Pallas kernels  83.1 us (94%)
  local copies, waits for them, and re-layouts  2.6 us (3%)
  between operations  1.3 us (1%)
  other arithmetic  1.24 us (1%)
    pallas_call x1, Pallas kernels, on_device(): pl.pallas_call(kernel, out_shape=jax.ShapeDtypeStruct((COLS, WIDTH), jnp....  83.1 us
    unnamed x5, local copies, waits for them, and re-layouts  2 us

profile of v1, /device:TPU:1, one launch (start us, length us, event | category | flops | bytes accessed | tf_op | source)
XLA Modules:
  0.0 88.2 jit_solution(7188742982260372811)
XLA Ops:
  0.0 0.0 copy-start
  0.0 0.0 copy-start.1
  0.0 0.7 copy-done
  0.7 0.1 constant_dynamic-slice_fusion
  0.8 0.5 fusion
  2.6 1.2 %broadcast_select_fusion.1 = (bf16[1,1,1,384,512]{4,3,2,1,0:T(8,128)(2,1)S(1)}, bf16[1,1,1,384,512]{4,3,2,1,0:T(8,128)(2,1)S(1)}) fusion(pred[]{:T(512)} %bitcast.1, bf16[1,1,2,384,512]{4,3,2,1,0:T(8,128)(2,1)} %param.4, pred[]{:T(512)} %bitcast.4), kind=kLoop, calls=%fused_computation.2 | loop fusion | flops 393216 | bytes 1572866 | tf_op jit(solution)/shard_map/jit(_where)/select_n | solution.py:192
  3.7 0.1 pad_maximum_fusion
  3.8 0.0 copy-done.1
  3.8 83.1 %shard_map.37 = bf16[2048,512]{1,0:T(8,128)(2,1)S(1)} custom-call(bf16[48,8192]{1,0:T(8,128)(2,1)S(1)} %bitcast.15, bf16[768,512]{1,0:T(8,128)(2,1)S(1)} %bitcast.14), custom_call_target="tpu_custom_call" | custom-call | tf_op jit(solution)/shard_map/pallas_call | solution.py:195
  86.9 1.3 %copy.7 = bf16[1,2048,512]{2,1,0:T(8,128)(2,1)} copy(bf16[1,2048,512]{2,1,0:T(8,128)(2,1)S(1)} %bitcast.13) | data formatting | bytes 4194304
Async XLA Ops:
  0.0 0.7 copy-start
  0.0 3.8 %copy-start.1 = (bf16[1,1,2,24,8192]{4,3,2,1,0:T(8,128)(2,1)S(1)}, bf16[1,1,2,24,8192]{4,3,2,1,0:T(8,128)(2,1)}, u32[]{:S(2)}) copy-start(bf16[1,1,2,24,8192]{4,3,2,1,0:T(8,128)(2,1)} %param.3) | copy-start | bytes 2359300

commit v2 on v0

v2 whole, which is shorter than its diff:
```python
import jax
import jax.numpy as jnp
from jax import lax
from jax.experimental import pallas as pl
from jax.experimental.pallas import tpu as pltpu
from jax.sharding import PartitionSpec as P

MESH = pl.DeviceIdType.MESH
N_DP, N_TENSOR, N_SECTION = 4, 16, 4
TOKENS = 24
PIECE = 2 * TOKENS
GROUP = 8 * PIECE
ROWS = N_TENSOR * PIECE
COLS = 2048
HALF = COLS // 2
WIDTH = 512
TILE = 2048
NEAR, FAR = 0, 1
RELAYED = (0, FAR)
ORDER = ((0, NEAR), (3, NEAR), (1, NEAR), (3, FAR), (2, NEAR), (1, FAR), (2, FAR), (0, FAR))
PARTS = 2


PLAN = (
    ("send", (0, NEAR)),
    ("send", (3, FAR)),
    ("send", (3, NEAR)),
    ("send", (1, FAR)),
    ("send", (1, NEAR)),
    ("send", (2, FAR)),
    ("send", (2, NEAR)),
    ("first", (0, NEAR)),
    ("first", (3, NEAR)),
    ("heads", None),
    ("first", (1, NEAR)),
    ("second", (0, NEAR)),
    ("first", (3, FAR)),
    ("second", (3, NEAR)),
    ("third", (0, NEAR)),
    ("first", (2, NEAR)),
    ("second", (1, NEAR)),
    ("third", (3, NEAR)),
    ("finish", (0, NEAR)),
    ("relay", None),
    ("first", (1, FAR)),
    ("second", (3, FAR)),
    ("third", (1, NEAR)),
    ("first", (2, FAR)),
    ("second", (2, NEAR)),
    ("third", (3, FAR)),
    ("heads2", None),
    ("finish", (3, NEAR)),
    ("first", (0, FAR)),
    ("second", (1, FAR)),
    ("third", (2, NEAR)),
    ("finish", (1, NEAR)),
    ("finish", (3, FAR)),
    ("second", (2, FAR)),
    ("third", (1, FAR)),
    ("second", (0, FAR)),
    ("third", (2, FAR)),
    ("heads3", None),
    ("finish", (2, NEAR)),
    ("finish", (1, FAR)),
    ("third", (0, FAR)),
    ("finish", (2, FAR)),
    ("finish", (0, FAR)),
)


def wrap(value, size):
    return lax.rem(value + size, size)


def kernel(
    order, grads, heads, out, a_all, b_all, acc, staged, heads_in, done,
    own_h, qs, qr, q1s, q1r, outs, s1s, s1r, rs, rr, x1s, x1r, x2s, x2r, dds, ddr, b1s, b1r, b2s, b2r,
):
    y = lax.axis_index("dp")
    t = lax.axis_index("tensor")
    s = lax.axis_index("section")
    x = lax.div(t, 4)
    h = lax.rem(lax.div(t, 2), 2)
    c = lax.rem(t, 2)
    z = 4 * h + s
    down, up = wrap(s - 1, 4), wrap(s + 1, 4)

    def tensor_of(xx, hh, cc):
        return xx * 4 + hh * 2 + cc

    def at_z(zz):
        return {"tensor": tensor_of(x, lax.div(zz, 4), c), "section": lax.rem(zz, 4)}

    to_z = (wrap(z - 1, 8), wrap(z + 3, 8))
    from_z = (wrap(z + 1, 8), wrap(z - 3, 8))
    from_h = tuple(lax.div(zz, 4) for zz in from_z)

    def rows_of(replica, xx, hh, cc):
        slot = replica * N_TENSOR + hh * 8 + xx * 2 + cc
        return pl.ds(pl.multiple_of(slot * PIECE, 16), PIECE)

    x_right, x_left, x_far = wrap(x + 1, 4), wrap(x - 1, 4), wrap(x + 2, 4)
    x_to = ({"tensor": tensor_of(x_right, h, c)}, {"tensor": tensor_of(x_left, h, c)})
    sibling = {"tensor": tensor_of(x, h, 1 - c)}
    y_up, y_down, y_far = wrap(y + 1, 4), wrap(y - 1, 4), wrap(y + 2, 4)
    y_to = ({"dp": y_up}, {"dp": y_down})

    own = pltpu.make_async_copy(heads, heads_in, own_h)
    own.start()

    barrier = pltpu.get_barrier_semaphore()

    def greet(device):
        pl.semaphore_signal(barrier, inc=1, device_id=device, device_id_type=MESH)

    for j in range(4):
        for n in (NEAR, FAR):
            if (j, n) != RELAYED:
                greet({"dp": wrap(y - j, 4), **at_z(from_z[n])})
    greet(at_z(wrap(z + 2, 8)))
    for device in (*x_to, sibling, *y_to):
        greet(device)
    pl.semaphore_wait(barrier, 13)

    def remote(src, dst, send, recv, device):
        return pltpu.make_async_remote_copy(
            src_ref=src, dst_ref=dst, send_sem=send, recv_sem=recv,
            device_id=device, device_id_type=MESH,
        )

    sends = []

    def go(copy):
        copy.start()
        sends.append(copy)

    def index(piece):
        return piece[0] * 2 + piece[1]

    def stage1(piece, part=None):
        j, n = piece
        target = wrap(y + j, 4)
        size = COLS if part is None else COLS // PARTS
        start = 0 if part is None else part * size
        return remote(
            grads.at[:, pl.ds(pl.multiple_of(target * COLS + start, size), size)],
            a_all.at[rows_of(y, x, h, c), pl.ds(start, size)],
            s1s.at[index(piece)] if part is None else qs.at[part],
            s1r.at[index(piece)] if part is None else qr.at[part],
            {"dp": target, **at_z(to_z[n])},
        )

    def stored(piece, xx, cc, half=None):
        j, n = piece
        rows = rows_of(wrap(y - j, 4), xx, from_h[n], cc)
        return a_all.at[rows, :] if half is None else a_all.at[rows, pl.ds(half * HALF, HALF)]

    def relay1():
        return remote(stored((RELAYED[0], NEAR), x, c), staged, rs.at[0], rr.at[0], at_z(wrap(z - 2, 8)))

    def relay2():
        rows = rows_of(wrap(y - RELAYED[0], 4), x, lax.div(wrap(z + 3, 8), 4), c)
        return remote(staged, a_all.at[rows, :], rs.at[1], rr.at[1], at_z(wrap(z - 2, 8)))

    def hop1(piece, way, xx, part=None):
        block = stored(piece, xx, c)
        if part is None:
            return remote(block, block, x1s.at[index(piece), way], x1r.at[index(piece), way], x_to[way])
        block = block.at[:, pl.ds(part * (COLS // PARTS), COLS // PARTS)]
        return remote(block, block, q1s.at[part, way], q1r.at[part, way], x_to[way])

    def hop2(piece, way, xx):
        block = stored(piece, xx, c, way)
        return remote(block, block, x2s.at[index(piece), way], x2r.at[index(piece), way], x_to[way])

    def across(piece, kind, cc):
        block = stored(piece, (x, x_left, x_right, x_far)[kind], cc)
        return remote(block, block, dds.at[index(piece), kind], ddr.at[index(piece), kind], sibling)

    def b_rows(replica, half=0, size=ROWS):
        return b_all.at[pl.ds(pl.multiple_of(replica * ROWS + half * (ROWS // 2), 128), size), :]

    def b_hop1(way, replica):
        block = b_rows(replica)
        return remote(block, block, b1s.at[way], b1r.at[way], y_to[way])

    def b_hop2(way, replica):
        block = b_rows(replica, way, ROWS // 2)
        return remote(block, block, b2s.at[way], b2r.at[way], y_to[way])

    def order_heads():
        own.wait()
        slots = (order[0, up], order[1, up])

        def place(slot, carry):
            source = tensor_of(lax.rem(lax.div(slot, 2), 4), lax.div(slot, 8), lax.rem(slot, 2))
            parts = [heads_in[m, source].astype(jnp.float32) for m in slots]
            rows = pl.ds(pl.multiple_of(y * ROWS + slot * PIECE, 16), PIECE)
            b_all[rows, :] = jnp.concatenate(parts, axis=0).astype(b_all.dtype)
            return carry

        lax.fori_loop(0, N_TENSOR, place, 0)

    def write(m):
        columns = pl.ds(pl.multiple_of(m * TILE, TILE), TILE)
        return pltpu.make_async_copy(done.at[columns, :], out.at[columns, :], outs.at[m])

    def compute(piece, first, last):
        j, n = piece
        start = wrap(y - j, 4) * ROWS + from_h[n] * GROUP
        rows = pl.ds(pl.multiple_of(start, GROUP), GROUP)

        def tile(m, carry):
            columns = pl.ds(pl.multiple_of(m * TILE, TILE), TILE)
            part = lax.dot_general(
                a_all[rows, columns], b_all[rows, :], (((0,), (0,)), ((), ())),
                preferred_element_type=jnp.float32,
            )
            if first:
                acc[columns, :] = part
            elif last:
                done[columns, :] = (acc[columns, :] + part).astype(done.dtype)
                write(m).start()
            else:
                acc[columns, :] += part
            return carry

        lax.fori_loop(0, COLS // TILE, tile, 0)

    def first(piece):
        if piece == ORDER[0]:
            for part in range(PARTS):
                stage1(piece, part).wait_recv()
                go(hop1(piece, 0, x, part))
                go(hop1(piece, 1, x, part))
            go(relay1())
        else:
            if piece == RELAYED:
                relay2().wait_recv()
            else:
                stage1(piece).wait_recv()
            go(hop1(piece, 0, x))
            go(hop1(piece, 1, x))
        go(across(piece, 0, c))

    def second(piece):
        for way, xx in ((0, x_left), (1, x_right)):
            if piece == ORDER[0]:
                for part in range(PARTS):
                    hop1(piece, way, xx, part).wait_recv()
            else:
                hop1(piece, way, xx).wait_recv()
            go(hop2(piece, way, xx))
            go(across(piece, 1 + way, c))

    def third(piece):
        hop2(piece, 0, x_far).wait_recv()
        hop2(piece, 1, x_far).wait_recv()
        go(across(piece, 3, c))

    def finish(piece):
        for kind in range(4):
            across(piece, kind, 1 - c).wait_recv()
        compute(piece, piece == ORDER[0], piece == ORDER[-1])

    paced = [piece for act, piece in PLAN if act == "sent"]
    for act, piece in PLAN:
        if act == "send":
            for copy in [stage1(piece, part) for part in range(PARTS)] if piece == ORDER[0] else [stage1(piece)]:
                copy.start()
                if piece not in paced:
                    sends.append(copy)
        elif act == "sent":
            stage1(piece).wait_send()
        elif act == "relay":
            relay1().wait_recv()
            go(relay2())
        elif act == "heads":
            order_heads()
            for way in (0, 1):
                go(b_hop1(way, y))
        elif act == "heads2":
            b_hop1(0, y_down).wait_recv()
            go(b_hop2(0, y_down))
            b_hop1(1, y_up).wait_recv()
            go(b_hop2(1, y_up))
        elif act == "heads3":
            for way in (0, 1):
                b_hop2(way, y_far).wait_recv()
        else:
            dict(first=first, second=second, third=third, finish=finish)[act](piece)
    for copy in sends:
        copy.wait_send()
    for m in range(COLS // TILE):
        write(m).wait()


def on_device(sent_grads, attn_out, b_order):
    grads = sent_grads[0, 0].reshape(PIECE, N_DP * COLS)
    heads = attn_out[0, 0].reshape(2, N_TENSOR, TOKENS, WIDTH)
    dma = pltpu.SemaphoreType.DMA
    result = pl.pallas_call(
        kernel,
        out_shape=jax.ShapeDtypeStruct((COLS, WIDTH), jnp.bfloat16),
        in_specs=[
            pl.BlockSpec(memory_space=pltpu.SMEM),
            pl.BlockSpec(memory_space=pltpu.HBM),
            pl.BlockSpec(memory_space=pltpu.HBM),
        ],
        out_specs=pl.BlockSpec(memory_space=pltpu.HBM),
        scratch_shapes=[
            pltpu.VMEM((N_DP * ROWS, COLS), jnp.bfloat16),
            pltpu.VMEM((N_DP * ROWS, WIDTH), jnp.bfloat16),
            pltpu.VMEM((COLS, WIDTH), jnp.float32),
            pltpu.VMEM((PIECE, COLS), jnp.bfloat16),
            pltpu.VMEM((2, N_TENSOR, TOKENS, WIDTH), jnp.bfloat16),
            pltpu.VMEM((COLS, WIDTH), jnp.bfloat16),
            dma, dma((PARTS,)), dma((PARTS,)), dma((PARTS, 2)), dma((PARTS, 2)), dma((COLS // TILE,)),
            dma((8,)), dma((8,)), dma((2,)), dma((2,)),
            dma((8, 2)), dma((8, 2)), dma((8, 2)), dma((8, 2)),
            dma((8, 4)), dma((8, 4)), dma((2,)), dma((2,)), dma((2,)), dma((2,)),
        ],
        compiler_params=pltpu.CompilerParams(
            collective_id=0, has_side_effects=True, vmem_limit_bytes=58 * 2**20
        ),
    )(b_order.T, grads, heads)
    return result[None]


def solution(mesh):
    placed = (
        P("section", "dp", None, "tensor", None),
        P("section", "dp", None, None, "tensor"),
        P(),
    )
    return jax.shard_map(
        on_device,
        mesh=mesh,
        in_specs=placed,
        out_specs=P("section", "dp", "tensor"),
        check_vma=False,
    )
```

time: 271 us -> 82.4 us (0.30)
  waiting for transfers between devices: 237 us -> 0 us
  Pallas kernels: 0 us -> 79.2 us
  matrix products: 13.7 us -> 0 us
  between operations: 13.4 us -> 0.01 us
  starting transfers between devices: 5.22 us -> 0 us
    all_gather x1 -> x0, waiting for transfers between devices: 144 us -> none  [on_device(): whole_grads = lax.all_gather(out_grads, 'tensor', axis=1, tiled=True)]
    pallas_call x0 -> x1, Pallas kernels: none -> 79.2 us  [on_device(): pl.pallas_call(kernel, out_shape=jax.ShapeDtypeStruct((COLS, WIDTH), jnp....]
    reduce_scatter x1 -> x0, waiting for transfers between devices: 77.4 us -> none  [on_device(): lax.psum_scatter(contract(whole_grads, heads_local).astype(jnp.bfloat16),...]
    ppermute x1 -> x0, waiting for transfers between devices: 15.7 us -> none  [from_behind(): return lax.ppermute(block, axis, route)]
    dot_general x1 -> x0, matrix products: 13.7 us -> none  [contract(): lax.dot_general(left_side, right_side, (((0, 1), (0, 1)), ((), ())), pref...]
    ppermute x1 -> x0, starting transfers between devices: 5.17 us -> none  [from_behind(): return lax.ppermute(block, axis, route)]
    unnamed x2 -> x1, local copies, waits for them, and re-layouts: 0.01 us -> 3.05 us
  transfers between devices with their start and end apart: 3 -> 0, of which waited for: 3 -> 0; matrix products, arithmetic and copies ran while one was open for 0% -> 0% of each run, Pallas kernels for 0% -> 0%
where the time goes in v2:
time: 82.4 us; the launch traced here: 82.3 us
  Pallas kernels  79.2 us (96%)
  local copies, waits for them, and re-layouts  3.05 us (4%)
    pallas_call x1, Pallas kernels, on_device(): pl.pallas_call(kernel, out_shape=jax.ShapeDtypeStruct((COLS, WIDTH), jnp....  79.2 us
    unnamed x1, local copies, waits for them, and re-layouts  3.05 us

profile of v2, /device:TPU:1, one launch (start us, length us, event | category | flops | bytes accessed | tf_op | source)
XLA Modules:
  0.0 82.3 jit_solution(12774444027413453219)
XLA Ops:
  0.0 79.2 %shard_map.37 = bf16[2048,512]{1,0:T(8,128)(2,1)} custom-call(s32[2,4]{1,0:T(2,128)} %bitcast.7, bf16[48,8192]{1,0:T(8,128)(2,1)} %bitcast.5, bf16[2,16,24,512]{3,2,1,0:T(8,128)(2,1)} %bitcast.6), custom_call_target="tpu_custom_call" | custom-call | tf_op jit(solution)/shard_map/pallas_call | solution.py:302
  79.2 3.0 %copy.5 = bf16[1,2048,512]{2,1,0:T(8,128)(2,1)} copy(bf16[1,2048,512]{2,1,0:T(8,128)(2,1)} %bitcast.4) | data formatting | bytes 4194304

commit v3 on v2

--- a/solution.py
+++ b/solution.py
@@ -32,26 +32,26 @@
     ("first", (0, NEAR)),
     ("first", (3, NEAR)),
     ("heads", None),
+    ("second", (0, NEAR)),
     ("first", (1, NEAR)),
-    ("second", (0, NEAR)),
+    ("second", (3, NEAR)),
     ("first", (3, FAR)),
-    ("second", (3, NEAR)),
     ("third", (0, NEAR)),
+    ("second", (1, NEAR)),
     ("first", (2, NEAR)),
-    ("second", (1, NEAR)),
     ("third", (3, NEAR)),
     ("finish", (0, NEAR)),
+    ("second", (3, FAR)),
+    ("first", (1, FAR)),
+    ("third", (1, NEAR)),
     ("relay", None),
-    ("first", (1, FAR)),
-    ("second", (3, FAR)),
-    ("third", (1, NEAR)),
+    ("second", (2, NEAR)),
     ("first", (2, FAR)),
-    ("second", (2, NEAR)),
     ("third", (3, FAR)),
     ("heads2", None),
     ("finish", (3, NEAR)),
+    ("second", (1, FAR)),
     ("first", (0, FAR)),
-    ("second", (1, FAR)),
     ("third", (2, NEAR)),
     ("finish", (1, NEAR)),
     ("finish", (3, FAR)),

time: 82.4 us -> 81.3 us (0.987)
  Pallas kernels: 79.2 us -> 78.2 us
    pallas_call x1, Pallas kernels: 79.2 us -> 78.2 us  [on_device(): pl.pallas_call(kernel, out_shape=jax.ShapeDtypeStruct((COLS, WIDTH), jnp....]
where the time goes in v3:
time: 81.3 us; the launch traced here: 81.2 us
  Pallas kernels  78.2 us (96%)
  local copies, waits for them, and re-layouts  3.05 us (4%)
    pallas_call x1, Pallas kernels, on_device(): pl.pallas_call(kernel, out_shape=jax.ShapeDtypeStruct((COLS, WIDTH), jnp....  78.2 us
    unnamed x1, local copies, waits for them, and re-layouts  3.05 us

profile of v3, /device:TPU:1, one launch (start us, length us, event | category | flops | bytes accessed | tf_op | source)
XLA Modules:
  0.0 81.2 jit_solution(5131379717723006217)
XLA Ops:
  0.0 78.2 %shard_map.37 = bf16[2048,512]{1,0:T(8,128)(2,1)} custom-call(s32[2,4]{1,0:T(2,128)} %bitcast.7, bf16[48,8192]{1,0:T(8,128)(2,1)} %bitcast.5, bf16[2,16,24,512]{3,2,1,0:T(8,128)(2,1)} %bitcast.6), custom_call_target="tpu_custom_call" | custom-call | tf_op jit(solution)/shard_map/pallas_call | solution.py:302
  78.2 3.0 %copy.5 = bf16[1,2048,512]{2,1,0:T(8,128)(2,1)} copy(bf16[1,2048,512]{2,1,0:T(8,128)(2,1)} %bitcast.4) | data formatting | bytes 4194304

commit v4 on v3

--- a/solution.py
+++ b/solution.py
@@ -54,15 +54,15 @@
     ("first", (0, FAR)),
     ("third", (2, NEAR)),
     ("finish", (1, NEAR)),
-    ("finish", (3, FAR)),
     ("second", (2, FAR)),
     ("third", (1, FAR)),
+    ("finish", (3, FAR)),
     ("second", (0, FAR)),
     ("third", (2, FAR)),
     ("heads3", None),
-    ("finish", (2, NEAR)),
     ("finish", (1, FAR)),
     ("third", (0, FAR)),
+    ("finish", (2, NEAR)),
     ("finish", (2, FAR)),
     ("finish", (0, FAR)),
 )

time: 81.3 us -> 80.9 us (level)
  no operation moved by 1% of the time
where the time goes in v4:
time: 80.9 us; the launch traced here: 80.5 us
  Pallas kernels  77.4 us (96%)
  local copies, waits for them, and re-layouts  3.05 us (4%)
    pallas_call x1, Pallas kernels, on_device(): pl.pallas_call(kernel, out_shape=jax.ShapeDtypeStruct((COLS, WIDTH), jnp....  77.4 us
    unnamed x1, local copies, waits for them, and re-layouts  3.05 us

profile of v4, /device:TPU:1, one launch (start us, length us, event | category | flops | bytes accessed | tf_op | source)
XLA Modules:
  0.0 80.5 jit_solution(7762993701788725918)
XLA Ops:
  0.0 77.4 %shard_map.37 = bf16[2048,512]{1,0:T(8,128)(2,1)} custom-call(s32[2,4]{1,0:T(2,128)} %bitcast.7, bf16[48,8192]{1,0:T(8,128)(2,1)} %bitcast.5, bf16[2,16,24,512]{3,2,1,0:T(8,128)(2,1)} %bitcast.6), custom_call_target="tpu_custom_call" | custom-call | tf_op jit(solution)/shard_map/pallas_call | solution.py:302
  77.4 3.0 %copy.5 = bf16[1,2048,512]{2,1,0:T(8,128)(2,1)} copy(bf16[1,2048,512]{2,1,0:T(8,128)(2,1)} %bitcast.4) | data formatting | bytes 4194304
